TPU v7x, 32 devices: a whole 2x2x4 slice. The times are simulated.
32 devices in a mesh: groups: 2 (over x), tm: 16 (over z, y, core).
Axes of the slice: x: 2, y: 2, z: 4, core: 2. Of those that a mesh axis runs over, the one named last changes fastest.
Arguments:
- latent: bfloat16 [64, 8192], P('groups', 'tm'), parts along dimension 0, may hold values from -6 to 6
- w_in: bfloat16 [3, 3, 3, 16, 384], replicated, may hold values from -0.3125 to 0.3125
- b_in: float32 [384], replicated, may hold values from -3 to 3
- gain: float32 [384], replicated, may hold values from 0.1 to 1.9
- w_mid: bfloat16 [3, 3, 3, 384, 384], replicated, may hold values from -0.0625 to 0.0625
- b_mid: float32 [384], replicated, may hold values from -3 to 3
- w_time: bfloat16 [3, 384, 768], replicated, may hold values from -0.1875 to 0.1875
- b_time: float32 [768], replicated, may hold values from -3 to 3
Outputs:
- frames_up: bfloat16 [128, 16, 32, 384], P(('groups', 'tm')), parts along dimension 0
There are 2 independent parts, one for each index of `groups`. A program takes and returns all parts, laid end to end along the dimension named above; an argument that names none is the same for every part. Nothing has to cross between parts.
All inputs are finite; a program needn't handle non-finite values.
Results may differ from a plain program's by a relative error of at most 0.012.
Values may be sent and summed in bfloat16 or wider, within the bound.
A program may use at most 128 MiB of HBM per device.

v0:
```python
import jax
import jax.numpy as jnp
from jax import lax
from jax.sharding import PartitionSpec as P

ZC = 16
C = 384
H = 16
W = 32


def passed_along(block, axis, distance):
    devices = range(lax.axis_size(axis))
    route = [(i - distance, i) for i in devices if i - distance in devices]
    return lax.ppermute(block, axis, route)


def conv_valid(padded, weight, bias, spatial):
    frames = padded.shape[0] - 2
    rows = padded.shape[1]
    inner = padded.shape[3]
    if spatial:
        margin = 1
        padded = jnp.pad(padded, ((0, 0), (1, 1), (margin, margin), (0, 0)))
        taps = 3
    else:
        taps = 1
    cols = padded.shape[2] - taps + 1
    total = jnp.zeros((frames * rows * cols, weight.shape[-1]), jnp.float32)
    for step_t in range(3):
        for step_h in range(taps):
            for step_w in range(taps):
                window = padded[
                    step_t : step_t + frames, step_h : step_h + rows, step_w : step_w + cols, :
                ]
                if spatial:
                    kernel = weight[step_t, step_h, step_w]
                else:
                    kernel = weight[step_t]
                total = total + jnp.dot(
                    window.reshape(-1, inner), kernel, preferred_element_type=jnp.float32
                )
    return (total + bias).reshape(frames, rows, cols, weight.shape[-1])


def conv_input(padded, weight, bias):
    frames = padded.shape[0] - 2
    rows = padded.shape[1]
    inner = padded.shape[3]
    margin = 1
    padded = jnp.pad(padded, ((0, 0), (1, 1), (margin, margin), (0, 0)))
    cols = padded.shape[2] - 2
    windows = []
    for step_t in range(3):
        for step_h in range(3):
            for step_w in range(3):
                windows.append(
                    padded[
                        step_t : step_t + frames, step_h : step_h + rows, step_w : step_w + cols, :
                    ]
                )
    stacked = jnp.concatenate(windows, axis=-1).reshape(frames * rows * cols, 27 * inner)
    total = jnp.dot(
        stacked, weight.reshape(27 * inner, weight.shape[-1]), preferred_element_type=jnp.float32
    )
    return (total + bias).reshape(frames, rows, cols, weight.shape[-1])


def activate(hidden, gain):
    values = hidden.astype(jnp.float32)
    scale = lax.rsqrt(jnp.mean(values * values, axis=-1, keepdims=True) + 1e-06)
    return jax.nn.silu(values * scale * gain).astype(jnp.bfloat16)


def per_device(latent, w_in, b_in, gain, w_mid, b_mid, w_time, b_time):
    owned = lax.all_to_all(latent, "tm", split_axis=0, concat_axis=1, tiled=True)
    frames = owned.shape[0]
    lat = owned.reshape(frames, H, W, ZC)
    earlier = passed_along(lat, "tm", 1)
    h0 = conv_input(jnp.concatenate([earlier, lat], axis=0), w_in, b_in).astype(jnp.bfloat16)
    act = activate(h0, gain)
    earlier_act = passed_along(act, "tm", 1)
    branch = conv_valid(jnp.concatenate([earlier_act, act], axis=0), w_mid, b_mid, True)
    h1 = (h0.astype(jnp.float32) + branch).astype(jnp.bfloat16)
    earlier_block = passed_along(h1, "tm", 1)
    up = conv_valid(jnp.concatenate([earlier_block, h1], axis=0), w_time, b_time, False)
    paired = up.reshape(frames, H, W, 2, C).transpose(0, 3, 1, 2, 4)
    return paired.reshape(2 * frames, H, W, C).astype(jnp.bfloat16)


def solution(mesh):
    return jax.shard_map(
        per_device,
        mesh=mesh,
        in_specs=(P("groups", "tm"), P(), P(), P(), P(), P(), P(), P()),
        out_specs=P(("groups", "tm"), None, None, None),
        check_vma=False,
    )
```

profile of v0, /device:TPU:8, one launch (start us, length us, event | category | flops | bytes accessed | tf_op | source)
XLA Modules:
  0.0 154.6 jit_solution(9824151615422119328)
XLA Ops:
  0.8 11.1 %all_to_all.16 = bf16[16,2,512]{2,1,0:T(2,128)(2,1)S(1)} all-to-all(bf16[16,2,512]{2,1,0:T(2,128)(2,1)S(1)} %all_to_all.12), channel_id=1, replica_groups=mesh['groups'=2,'tm'=16] {'tm'}, dimensions={0} | all-to-all | bytes 65536 | tf_op jit(solution)/shard_map/all_to_all | solution.py:76
  12.2 2.0 %collective-permute-start = (bf16[2,16,32,16]{3,2,1,0:T(8,128)(2,1)S(1)}, bf16[2,16,32,16]{3,2,1,0:T(8,128)(2,1)S(1)}, u32[]{:S(2)}, u32[]{:S(2)}) collective-permute-start(bf16[2,16,32,16]{3,2,1,0:T(8,128)(2,1)S(1)} %reshape.157), channel_id=1, source_target_pairs={{0,1},{1,2},{2,3},{3,4},{4,5},{5,6},{6,7},{7,8},{8,9},{9,10},{10,1... | collective-permute-start | bytes 98312 | tf_op jit(solution)/shard_map/ppermute | solution.py:15
  14.6 6.2 %collective-permute-done = bf16[2,16,32,16]{3,2,1,0:T(8,128)(2,1)S(1)} collective-permute-done((bf16[2,16,32,16]{3,2,1,0:T(8,128)(2,1)S(1)}, bf16[2,16,32,16]{3,2,1,0:T(8,128)(2,1)S(1)}, u32[]{:S(2)}, u32[]{:S(2)}) %collective-permute-start) | collective-permute-done | bytes 32800 | tf_op jit(solution)/shard_map/ppermute | solution.py:15
  21.2 2.5 %pad_slice_fusion.26 = (bf16[2,16,32,16]{3,2,1,0:T(8,128)(2,1)}, bf16[2,16,32,16]{3,2,1,0:T(8,128)(2,1)}, bf16[2,16,32,16]{3,2,1,0:T(8,128)(2,1)}, bf16[2,16,32,...) fusion(bf16[4,16,32,16]{3,2,1,0:T(8,128)(2,1)S(1)} %constant_dy, ...), kind=kLoop, calls=%fused_computation.36 | loop fusion | bytes 688128 | tf_op jit(solution)/shard_map/slice | solution.py:58
  58.4 2.0 %multiply_reduce_fusion = (f32[1024]{0:T(1024)S(1)}, f32[1024,384]{1,0:T(8,128)S(1)}) fusion(f32[384]{0:T(512)S(1)} %copy-done.44, bf16[1024,432]{0,1:T(8,128)(2,1)} %constant_dynamic-update-slice_fusion.2, bf16[432,384]{1,0:T(8,128)(2,1)S(1)} %bitcast.180), kind=kOutput, calls=%fused_computation.33 | convolution fusion | flops 341703680 | bytes 2795008 | tf_op jit(solution)/shard_map/dot_general | solution.py:63
  61.0 1.9 %collective-permute-start.1 = (bf16[2,16,32,384]{3,2,1,0:T(8,128)(2,1)S(1)}, bf16[2,16,32,384]{3,2,1,0:T(8,128)(2,1)S(1)}, u32[]{:S(2)}, u32[]{:S(2)}) collective-permute-start(bf16[2,16,32,384]{3,2,1,0:T(8,128)(2,1)S(1)} %multiply_convert_fusion.1), channel_id=1, source_target_pairs={{0,1},{1,2},{2,3},{3,4},{4,5},{5,6},{6,7},{7,8},{8,9},{9,10},{10,1... | collective-permute-start | bytes 2359304 | tf_op jit(solution)/shard_map/ppermute | solution.py:15
  62.9 3.0 %fusion.3 = f32[1024,384]{1,0:T(8,128)} fusion(f32[1024,384]{1,0:T(8,128)S(1)} %get-tuple-element.55, f32[384]{0:T(512)S(1)} %copy-done.43, f32[1024]{0:T(1024)S(1)} %add_rsqrt_fusion, bf16[3,3,3,384,384]{4,3,2,1,0:T(8,128)(2,1)} %param.12), kind=kOutput, calls=%fused_computation.63 | convolution fusion | flops 304742400 | bytes 3446272 | tf_op jit(solution)/shard_map/dot_general | solution.py:40
  65.9 9.3 %collective-permute-done.1 = bf16[2,16,32,384]{3,2,1,0:T(8,128)(2,1)S(1)} collective-permute-done((bf16[2,16,32,384]{3,2,1,0:T(8,128)(2,1)S(1)}, bf16[2,16,32,384]{3,2,1,0:T(8,128)(2,1)S(1)}, u32[]{:S(2)}, u32[]{:S(2)}) %collective-permute-start.1) | collective-permute-done | bytes 786464 | tf_op jit(solution)/shard_map/ppermute | solution.py:15
  75.4 2.1 %pad_slice_fusion.23 = (bf16[2,16,32,384]{3,2,1,0:T(8,128)(2,1)S(1)}, bf16[2,16,32,384]{3,2,1,0:T(8,128)(2,1)S(1)}, bf16[2,16,32,384]{3,2,1,0:T(8,128)(2,1)S(1)}...) fusion(bf16[4,16,32,384]{3,2,1,0:T(8,128)(2,1)S(1)} %pad_maximum_fusion), kind=kLoop, calls=%fused_computation.23 | loop fusion | bytes 5505024 | tf_op jit(solution)/shard_map/slice | solution.py:33
  77.5 6.2 %pad_slice_fusion = (bf16[2,16,32,384]{3,2,1,0:T(8,128)(2,1)}, bf16[2,16,32,384]{3,2,1,0:T(8,128)(2,1)}, bf16[2,16,32,384]{3,2,1,0:T(8,128)(2,1)}, bf16[2,16,32,...) fusion(bf16[4,16,32,384]{3,2,1,0:T(8,128)(2,1)S(1)} %pad_maximu, ...), kind=kLoop, calls=%fused_computation | loop fusion | bytes 16515072 | tf_op jit(solution)/shard_map/slice | solution.py:33
  88.3 1.8 %fusion.12 = f32[1024,384]{1,0:T(8,128)} fusion(bf16[1024,384]{1,0:T(8,128)(2,1)S(1)} %bitcast.210, bf16[3,3,3,384,384]{4,3,2,1,0:T(8,128)(2,1)S(1)} %bitcast.185), kind=kOutput, calls=%fused_computation.72 | convolution fusion | flops 301989888 | bytes 2654208 | tf_op jit(solution)/shard_map/dot_general | solution.py:40
  90.0 1.8 %fusion.59 = f32[1024,384]{1,0:T(8,128)} fusion(bf16[1024,384]{1,0:T(8,128)(2,1)S(1)} %bitcast.205, bf16[3,3,3,384,384]{4,3,2,1,0:T(8,128)(2,1)S(1)} %bitcast.185), kind=kOutput, calls=%fused_computation.119 | convolution fusion | flops 301989888 | bytes 2654208 | tf_op jit(solution)/shard_map/dot_general | solution.py:40
  91.8 1.8 %fusion.57 = f32[1024,384]{1,0:T(8,128)} fusion(bf16[1024,384]{1,0:T(8,128)(2,1)S(1)} %bitcast.204, bf16[3,3,3,384,384]{4,3,2,1,0:T(8,128)(2,1)S(1)} %bitcast.185), kind=kOutput, calls=%fused_computation.117 | convolution fusion | flops 301989888 | bytes 2654208 | tf_op jit(solution)/shard_map/dot_general | solution.py:40
  93.6 1.8 %fusion.55 = f32[1024,384]{1,0:T(8,128)} fusion(bf16[1024,384]{1,0:T(8,128)(2,1)S(1)} %bitcast.203, bf16[3,3,3,384,384]{4,3,2,1,0:T(8,128)(2,1)S(1)} %bitcast.185), kind=kOutput, calls=%fused_computation.115 | convolution fusion | flops 301989888 | bytes 2654208 | tf_op jit(solution)/shard_map/dot_general | solution.py:40
  95.4 1.8 %fusion.51 = f32[1024,384]{1,0:T(8,128)} fusion(bf16[1024,384]{1,0:T(8,128)(2,1)S(1)} %bitcast.202, bf16[3,3,3,384,384]{4,3,2,1,0:T(8,128)(2,1)S(1)} %bitcast.185), kind=kOutput, calls=%fused_computation.111 | convolution fusion | flops 301989888 | bytes 2654208 | tf_op jit(solution)/shard_map/dot_general | solution.py:40
  97.2 1.8 %fusion.49 = f32[1024,384]{1,0:T(8,128)} fusion(bf16[1024,384]{1,0:T(8,128)(2,1)S(1)} %bitcast.201, bf16[3,3,3,384,384]{4,3,2,1,0:T(8,128)(2,1)S(1)} %bitcast.185), kind=kOutput, calls=%fused_computation.109 | convolution fusion | flops 301989888 | bytes 2654208 | tf_op jit(solution)/shard_map/dot_general | solution.py:40
  99.1 1.8 %fusion.47 = f32[1024,384]{1,0:T(8,128)} fusion(bf16[1024,384]{1,0:T(8,128)(2,1)S(1)} %bitcast.200, bf16[3,3,3,384,384]{4,3,2,1,0:T(8,128)(2,1)S(1)} %bitcast.185), kind=kOutput, calls=%fused_computation.107 | convolution fusion | flops 301989888 | bytes 2654208 | tf_op jit(solution)/shard_map/dot_general | solution.py:40
  100.9 1.9 %fusion.45 = f32[1024,384]{1,0:T(8,128)} fusion(bf16[1024,384]{1,0:T(8,128)(2,1)S(1)} %bitcast.199, bf16[3,3,3,384,384]{4,3,2,1,0:T(8,128)(2,1)S(1)} %bitcast.185), kind=kOutput, calls=%fused_computation.105 | convolution fusion | flops 301989888 | bytes 2654208 | tf_op jit(solution)/shard_map/dot_general | solution.py:40
  102.7 1.8 %fusion.43 = f32[1024,384]{1,0:T(8,128)} fusion(bf16[1024,384]{1,0:T(8,128)(2,1)S(1)} %bitcast.198, bf16[3,3,3,384,384]{4,3,2,1,0:T(8,128)(2,1)S(1)} %bitcast.185), kind=kOutput, calls=%fused_computation.103 | convolution fusion | flops 301989888 | bytes 2654208 | tf_op jit(solution)/shard_map/dot_general | solution.py:40
  104.5 1.8 %fusion.41 = f32[1024,384]{1,0:T(8,128)} fusion(bf16[1024,384]{1,0:T(8,128)(2,1)S(1)} %bitcast.197, bf16[3,3,3,384,384]{4,3,2,1,0:T(8,128)(2,1)S(1)} %bitcast.185), kind=kOutput, calls=%fused_computation.101 | convolution fusion | flops 301989888 | bytes 2654208 | tf_op jit(solution)/shard_map/dot_general | solution.py:40
  106.3 1.8 %fusion.39 = f32[1024,384]{1,0:T(8,128)} fusion(bf16[1024,384]{1,0:T(8,128)(2,1)S(1)} %bitcast.196, bf16[3,3,3,384,384]{4,3,2,1,0:T(8,128)(2,1)S(1)} %bitcast.185), kind=kOutput, calls=%fused_computation.99 | convolution fusion | flops 301989888 | bytes 2654208 | tf_op jit(solution)/shard_map/dot_general | solution.py:40
  108.1 1.8 %fusion.37 = f32[1024,384]{1,0:T(8,128)} fusion(bf16[1024,384]{1,0:T(8,128)(2,1)S(1)} %bitcast.195, bf16[3,3,3,384,384]{4,3,2,1,0:T(8,128)(2,1)S(1)} %bitcast.185), kind=kOutput, calls=%fused_computation.97 | convolution fusion | flops 301989888 | bytes 2654208 | tf_op jit(solution)/shard_map/dot_general | solution.py:40
  109.9 1.8 %fusion.33 = f32[1024,384]{1,0:T(8,128)} fusion(bf16[1024,384]{1,0:T(8,128)(2,1)S(1)} %bitcast.194, bf16[3,3,3,384,384]{4,3,2,1,0:T(8,128)(2,1)S(1)} %bitcast.185), kind=kOutput, calls=%fused_computation.93 | convolution fusion | flops 301989888 | bytes 2654208 | tf_op jit(solution)/shard_map/dot_general | solution.py:40
  111.6 1.8 %fusion.31 = f32[1024,384]{1,0:T(8,128)} fusion(bf16[1024,384]{1,0:T(8,128)(2,1)S(1)} %bitcast.193, bf16[3,3,3,384,384]{4,3,2,1,0:T(8,128)(2,1)S(1)} %bitcast.185), kind=kOutput, calls=%fused_computation.91 | convolution fusion | flops 301989888 | bytes 2654208 | tf_op jit(solution)/shard_map/dot_general | solution.py:40
  113.5 2.1 %fusion.29 = f32[1024,384]{1,0:T(8,128)} fusion(bf16[1024,384]{1,0:T(8,128)(2,1)S(1)} %bitcast.192, bf16[3,3,3,384,384]{4,3,2,1,0:T(8,128)(2,1)S(1)} %bitcast.185), kind=kOutput, calls=%fused_computation.89 | convolution fusion | flops 301989888 | bytes 2654208 | tf_op jit(solution)/shard_map/dot_general | solution.py:40
  115.5 1.9 %fusion.27 = f32[1024,384]{1,0:T(8,128)} fusion(bf16[1024,384]{1,0:T(8,128)(2,1)S(1)} %bitcast.191, bf16[3,3,3,384,384]{4,3,2,1,0:T(8,128)(2,1)S(1)} %bitcast.185), kind=kOutput, calls=%fused_computation.87 | convolution fusion | flops 301989888 | bytes 2654208 | tf_op jit(solution)/shard_map/dot_general | solution.py:40
  117.4 1.9 %fusion.25 = f32[1024,384]{1,0:T(8,128)} fusion(bf16[1024,384]{1,0:T(8,128)(2,1)S(1)} %bitcast.190, bf16[3,3,3,384,384]{4,3,2,1,0:T(8,128)(2,1)S(1)} %bitcast.185), kind=kOutput, calls=%fused_computation.85 | convolution fusion | flops 301989888 | bytes 2654208 | tf_op jit(solution)/shard_map/dot_general | solution.py:40
  119.3 1.8 %fusion.23 = f32[1024,384]{1,0:T(8,128)} fusion(bf16[1024,384]{1,0:T(8,128)(2,1)S(1)} %bitcast.189, bf16[3,3,3,384,384]{4,3,2,1,0:T(8,128)(2,1)S(1)} %bitcast.185), kind=kOutput, calls=%fused_computation.83 | convolution fusion | flops 301989888 | bytes 2654208 | tf_op jit(solution)/shard_map/dot_general | solution.py:40
  121.0 1.8 %fusion.21 = f32[1024,384]{1,0:T(8,128)} fusion(bf16[1024,384]{1,0:T(8,128)(2,1)S(1)} %bitcast.188, bf16[3,3,3,384,384]{4,3,2,1,0:T(8,128)(2,1)S(1)} %bitcast.185), kind=kOutput, calls=%fused_computation.81 | convolution fusion | flops 301989888 | bytes 2654208 | tf_op jit(solution)/shard_map/dot_general | solution.py:40
  122.8 13.2 %add_add_fusion = f32[1024,384]{1,0:T(8,128)S(1)} fusion(f32[1024,384]{1,0:T(8,128)} %fusion.12, f32[1024,384]{1,0:T(8,128)S(1)} %fusion.14, f32[1024,384]{1,0:T(8,128)S(1)} %fusion.16, f32[1024,384]{1,0:T(8,128)} %fusion.3, f32[1024,384]{1,0:T(8,128)S(1)} %fusion.19, f32[1024,384]{1,0:T(8,128)} %fusion.21, f32[1024,384]{1,0:T(8,128)} %fusion.23, ...), kind=kOutput, calls=%fused_computation.30 | convolution fusion | flops 312606720 | bytes 43550208 | tf_op jit(solution)/shard_map/dot_general | solution.py:40
  136.3 2.1 %collective-permute-start.2 = (bf16[2,16,32,384]{3,2,1,0:T(8,128)(2,1)S(1)}, bf16[2,16,32,384]{3,2,1,0:T(8,128)(2,1)S(1)}, u32[]{:S(2)}, u32[]{:S(2)}) collective-permute-start(bf16[2,16,32,384]{3,2,1,0:T(8,128)(2,1)S(1)} %add_convert_fusion.2), channel_id=1, source_target_pairs={{0,1},{1,2},{2,3},{3,4},{4,5},{5,6},{6,7},{7,8},{8,9},{9,10},{10,1... | collective-permute-start | bytes 2359304 | tf_op jit(solution)/shard_map/ppermute | solution.py:15
  139.4 11.3 %collective-permute-done.2 = bf16[2,16,32,384]{3,2,1,0:T(8,128)(2,1)S(1)} collective-permute-done((bf16[2,16,32,384]{3,2,1,0:T(8,128)(2,1)S(1)}, bf16[2,16,32,384]{3,2,1,0:T(8,128)(2,1)S(1)}, u32[]{:S(2)}, u32[]{:S(2)}) %collective-permute-start.2) | collective-permute-done | bytes 786464 | tf_op jit(solution)/shard_map/ppermute | solution.py:15
  (174 shorter events, 46.7 us)
Async XLA Ops:
  0.0 58.4 %copy-start = (bf16[3,3,3,16,384]{4,3,2,1,0:T(8,128)(2,1)S(1)}, bf16[3,3,3,16,384]{4,3,2,1,0:T(8,128)(2,1)}, u32[]{:S(2)}) copy-start(bf16[3,3,3,16,384]{4,3,2,1,0:T(8,128)(2,1)} %param.9) | copy-start | bytes 995332
  12.2 8.6 %collective-permute-start = (bf16[2,16,32,16]{3,2,1,0:T(8,128)(2,1)S(1)}, bf16[2,16,32,16]{3,2,1,0:T(8,128)(2,1)S(1)}, u32[]{:S(2)}, u32[]{:S(2)}) collective-permute-start(bf16[2,16,32,16]{3,2,1,0:T(8,128)(2,1)S(1)} %reshape.157), channel_id=1, source_target_pairs={{0,1},{1,2},{2,3},{3,4},{4,5},{5,6},{6,7},{7,8},{8,9},{9,10},{10,1... | collective-permute-start | bytes 98312 | tf_op jit(solution)/shard_map/ppermute | solution.py:15
  26.0 14.0 %copy-start.27 = (bf16[2,16,32,16]{3,2,1,0:T(8,128)(2,1)S(1)}, bf16[2,16,32,16]{3,2,1,0:T(8,128)(2,1)}, u32[]{:S(2)}) copy-start(bf16[2,16,32,16]{3,2,1,0:T(8,128)(2,1)} %get-tuple-element.36) | copy-start | bytes 98308
  26.8 14.0 %copy-start.26 = (bf16[2,16,32,16]{3,2,1,0:T(8,128)(2,1)S(1)}, bf16[2,16,32,16]{3,2,1,0:T(8,128)(2,1)}, u32[]{:S(2)}) copy-start(bf16[2,16,32,16]{3,2,1,0:T(8,128)(2,1)} %get-tuple-element.37) | copy-start | bytes 98308
  27.5 13.4 %copy-start.25 = (bf16[2,16,32,16]{3,2,1,0:T(8,128)(2,1)S(1)}, bf16[2,16,32,16]{3,2,1,0:T(8,128)(2,1)}, u32[]{:S(2)}) copy-start(bf16[2,16,32,16]{3,2,1,0:T(8,128)(2,1)} %get-tuple-element.38) | copy-start | bytes 98308
  27.6 13.5 %copy-start.24 = (bf16[2,16,32,16]{3,2,1,0:T(8,128)(2,1)S(1)}, bf16[2,16,32,16]{3,2,1,0:T(8,128)(2,1)}, u32[]{:S(2)}) copy-start(bf16[2,16,32,16]{3,2,1,0:T(8,128)(2,1)} %get-tuple-element.39) | copy-start | bytes 98308
  28.3 13.0 %copy-start.23 = (bf16[2,16,32,16]{3,2,1,0:T(8,128)(2,1)S(1)}, bf16[2,16,32,16]{3,2,1,0:T(8,128)(2,1)}, u32[]{:S(2)}) copy-start(bf16[2,16,32,16]{3,2,1,0:T(8,128)(2,1)} %get-tuple-element.40) | copy-start | bytes 98308
  30.0 11.4 %copy-start.22 = (bf16[2,16,32,16]{3,2,1,0:T(8,128)(2,1)S(1)}, bf16[2,16,32,16]{3,2,1,0:T(8,128)(2,1)}, u32[]{:S(2)}) copy-start(bf16[2,16,32,16]{3,2,1,0:T(8,128)(2,1)} %get-tuple-element.41) | copy-start | bytes 98308
  31.7 9.8 %copy-start.21 = (bf16[2,16,32,16]{3,2,1,0:T(8,128)(2,1)S(1)}, bf16[2,16,32,16]{3,2,1,0:T(8,128)(2,1)}, u32[]{:S(2)}) copy-start(bf16[2,16,32,16]{3,2,1,0:T(8,128)(2,1)} %get-tuple-element.42) | copy-start | bytes 98308
  40.9 2.0 %copy-start.40 = (bf16[1024,16]{0,1:T(8,128)(2,1)S(1)}, bf16[1024,16]{0,1:T(8,128)(2,1)}, u32[]{:S(2)}) copy-start(bf16[1024,16]{0,1:T(8,128)(2,1)} %copy.71) | copy-start | bytes 98308
  40.9 2.6 %copy-start.38 = (bf16[1024,16]{0,1:T(8,128)(2,1)S(1)}, bf16[1024,16]{0,1:T(8,128)(2,1)}, u32[]{:S(2)}) copy-start(bf16[1024,16]{0,1:T(8,128)(2,1)} %copy.72) | copy-start | bytes 98308
  41.0 3.2 %copy-start.33 = (bf16[1024,16]{0,1:T(8,128)(2,1)S(1)}, bf16[1024,16]{0,1:T(8,128)(2,1)}, u32[]{:S(2)}) copy-start(bf16[1024,16]{0,1:T(8,128)(2,1)} %copy.73) | copy-start | bytes 98308
  41.0 3.8 %copy-start.37 = (bf16[1024,16]{0,1:T(8,128)(2,1)S(1)}, bf16[1024,16]{0,1:T(8,128)(2,1)}, u32[]{:S(2)}) copy-start(bf16[1024,16]{0,1:T(8,128)(2,1)} %copy.74) | copy-start | bytes 98308
  41.1 4.3 %copy-start.36 = (bf16[1024,16]{0,1:T(8,128)(2,1)S(1)}, bf16[1024,16]{0,1:T(8,128)(2,1)}, u32[]{:S(2)}) copy-start(bf16[1024,16]{0,1:T(8,128)(2,1)} %copy.75) | copy-start | bytes 98308
  41.1 4.9 %copy-start.35 = (bf16[1024,16]{0,1:T(8,128)(2,1)S(1)}, bf16[1024,16]{0,1:T(8,128)(2,1)}, u32[]{:S(2)}) copy-start(bf16[1024,16]{0,1:T(8,128)(2,1)} %copy.76) | copy-start | bytes 98308
  41.1 5.5 %copy-start.34 = (bf16[1024,16]{0,1:T(8,128)(2,1)S(1)}, bf16[1024,16]{0,1:T(8,128)(2,1)}, u32[]{:S(2)}) copy-start(bf16[1024,16]{0,1:T(8,128)(2,1)} %copy.77) | copy-start | bytes 98308
  41.2 8.5 %copy-start.32 = (bf16[1024,16]{0,1:T(8,128)(2,1)S(1)}, bf16[1024,16]{0,1:T(8,128)(2,1)}, u32[]{:S(2)}) copy-start(bf16[1024,16]{0,1:T(8,128)(2,1)} %copy.82) | copy-start | bytes 98308
  41.5 13.2 %copy-start.31 = (bf16[1024,16]{0,1:T(8,128)(2,1)S(1)}, bf16[1024,16]{0,1:T(8,128)(2,1)}, u32[]{:S(2)}) copy-start(bf16[1024,16]{0,1:T(8,128)(2,1)} %copy.90) | copy-start | bytes 98308
  41.5 14.4 %copy-start.29 = (bf16[1024,16]{0,1:T(8,128)(2,1)S(1)}, bf16[1024,16]{0,1:T(8,128)(2,1)}, u32[]{:S(2)}) copy-start(bf16[1024,16]{0,1:T(8,128)(2,1)} %copy.91) | copy-start | bytes 98308
  41.6 14.9 %copy-start.28 = (bf16[1024,16]{0,1:T(8,128)(2,1)S(1)}, bf16[1024,16]{0,1:T(8,128)(2,1)}, u32[]{:S(2)}) copy-start(bf16[1024,16]{0,1:T(8,128)(2,1)} %copy.92) | copy-start | bytes 98308
  41.6 16.1 %copy-start.30 = (bf16[1024,16]{0,1:T(8,128)(2,1)S(1)}, bf16[1024,16]{0,1:T(8,128)(2,1)}, u32[]{:S(2)}) copy-start(bf16[1024,16]{0,1:T(8,128)(2,1)} %copy.94) | copy-start | bytes 98308
  41.6 16.7 %copy-start.44 = (f32[384]{0:T(512)S(1)}, f32[384]{0:T(512)}, u32[]{:S(2)}) copy-start(f32[384]{0:T(512)} %param.10) | copy-start | bytes 4612
  58.4 2.1 %copy-start.43 = (f32[384]{0:T(512)S(1)}, f32[384]{0:T(512)}, u32[]{:S(2)}) copy-start(f32[384]{0:T(512)} %param.11) | copy-start | bytes 4612
  61.0 14.2 %collective-permute-start.1 = (bf16[2,16,32,384]{3,2,1,0:T(8,128)(2,1)S(1)}, bf16[2,16,32,384]{3,2,1,0:T(8,128)(2,1)S(1)}, u32[]{:S(2)}, u32[]{:S(2)}) collective-permute-start(bf16[2,16,32,384]{3,2,1,0:T(8,128)(2,1)S(1)} %multiply_convert_fusion.1), channel_id=1, source_target_pairs={{0,1},{1,2},{2,3},{3,4},{4,5},{5,6},{6,7},{7,8},{8,9},{9,10},{10,1... | collective-permute-start | bytes 2359304 | tf_op jit(solution)/shard_map/ppermute | solution.py:15
  75.4 8.5 %slice-start = ((s8[7962624]{0:T(1024)(128)(4,1)}), s8[4194304]{0:T(1024)(128)(4,1)S(1)}, s32[]{:S(2)}) async-start(s8[7962624]{0:T(1024)(128)(4,1)} %bitcast.184), calls=%async_computation.1 | async-start | bytes 8388608
  77.5 6.3 %slice-start.1 = ((s8[7962624]{0:T(1024)(128)(4,1)}), s8[3768320]{0:T(1024)(128)(4,1)S(1)}, s32[]{:S(2)}) async-start(s8[7962624]{0:T(1024)(128)(4,1)} %bitcast.184), calls=%async_computation.2 | async-start | bytes 7536640
  97.2 1.8 %copy-start.12 = (bf16[2,16,32,384]{3,2,1,0:T(8,128)(2,1)S(1)}, bf16[2,16,32,384]{3,2,1,0:T(8,128)(2,1)}, u32[]{:S(2)}) copy-start(bf16[2,16,32,384]{3,2,1,0:T(8,128)(2,1)} %get-tuple-element.11) | copy-start | bytes 2359300
  100.8 1.9 %copy-start.10 = (bf16[2,16,32,384]{3,2,1,0:T(8,128)(2,1)S(1)}, bf16[2,16,32,384]{3,2,1,0:T(8,128)(2,1)}, u32[]{:S(2)}) copy-start(bf16[2,16,32,384]{3,2,1,0:T(8,128)(2,1)} %get-tuple-element.13) | copy-start | bytes 2359300
  113.5 2.1 %copy-start.3 = (bf16[2,16,32,384]{3,2,1,0:T(8,128)(2,1)S(1)}, bf16[2,16,32,384]{3,2,1,0:T(8,128)(2,1)}, u32[]{:S(2)}) copy-start(bf16[2,16,32,384]{3,2,1,0:T(8,128)(2,1)} %get-tuple-element.20) | copy-start | bytes 2359300
  115.5 1.9 %copy-start.2 = (bf16[2,16,32,384]{3,2,1,0:T(8,128)(2,1)S(1)}, bf16[2,16,32,384]{3,2,1,0:T(8,128)(2,1)}, u32[]{:S(2)}) copy-start(bf16[2,16,32,384]{3,2,1,0:T(8,128)(2,1)} %get-tuple-element.21) | copy-start | bytes 2359300
  136.0 2.4 %copy-start.20 = (bf16[3,384,768]{2,1,0:T(8,128)(2,1)S(1)}, bf16[3,384,768]{2,1,0:T(8,128)(2,1)}, u32[]{:S(2)}) copy-start(bf16[3,384,768]{2,1,0:T(8,128)(2,1)} %param.14) | copy-start | bytes 5308420
  136.3 14.3 %collective-permute-start.2 = (bf16[2,16,32,384]{3,2,1,0:T(8,128)(2,1)S(1)}, bf16[2,16,32,384]{3,2,1,0:T(8,128)(2,1)S(1)}, u32[]{:S(2)}, u32[]{:S(2)}) collective-permute-start(bf16[2,16,32,384]{3,2,1,0:T(8,128)(2,1)S(1)} %add_convert_fusion.2), channel_id=1, source_target_pairs={{0,1},{1,2},{2,3},{3,4},{4,5},{5,6},{6,7},{7,8},{8,9},{9,10},{10,1... | collective-permute-start | bytes 2359304 | tf_op jit(solution)/shard_map/ppermute | solution.py:15
  (18 other events, 29.6 us)
where the time goes:
time: 155 us
  matrix products  59.3 us (38%)
  local copies, waits for them, and re-layouts  49.7 us (32%)
  waiting for transfers between devices  26.8 us (17%)
  blocking collectives  11.1 us (7%)
  starting transfers between devices  6 us (4%)
    dot_general x30, matrix products, conv_valid(): jnp.dot(window.reshape(-1, inner), kernel, preferred_element_type=jnp.flo...  57.3 us
    ppermute x3, waiting for transfers between devices, passed_along(): return lax.ppermute(block, axis, route)  26.8 us
    concatenate x29, local copies, waits for them, and re-layouts, conv_input(): jnp.concatenate(windows, axis=-1).reshape(frames * rows * cols, 27 * inner)  18.7 us
    unnamed x121, local copies, waits for them, and re-layouts  16.8 us
    all_to_all x1, blocking collectives, per_device(): lax.all_to_all(latent, 'tm', split_axis=0, concat_axis=1, tiled=True)  11.1 us
    slice x2, local copies, waits for them, and re-layouts, conv_valid(): padded[step_t:step_t + frames, step_h:step_h + rows, step_w:step_w + cols...  8.35 us
    ppermute x3, starting transfers between devices, passed_along(): return lax.ppermute(block, axis, route)  6 us
  transfers between devices with their start and end apart: 3, of which 3 were waited for; matrix products, arithmetic and copies ran while one was open for 3% of the time, Pallas kernels for 0%

commit v1 on v0

--- a/solution.py
+++ b/solution.py
@@ -7,6 +7,28 @@
 C = 384
 H = 16
 W = 32
+
+
+def in_blocks(shard, dim, size):
+    before, after = (shard.shape[:dim], shard.shape[dim + 1 :])
+    return jnp.moveaxis(shard.reshape(*before, size, -1, *after), dim, 0)
+
+
+def in_order(tiles, dim):
+    tiles = jnp.moveaxis(tiles, 0, dim)
+    shape = tiles.shape
+    return tiles.reshape(*shape[:dim], shape[dim] * shape[dim + 1], *shape[dim + 2 :])
+
+
+def exchange_in_pairs(value, axis, split_dim, concat_dim):
+    size, place = (lax.axis_size(axis), lax.axis_index(axis))
+    blocks = in_blocks(value, split_dim, size)
+    outs = [blocks[place]]
+    for step in range(1, size):
+        sent = blocks[place ^ step]
+        outs.append(lax.ppermute(sent, axis, [(i, i ^ step) for i in range(size)]))
+    blocks = jnp.stack(outs)[place ^ jnp.arange(size)]
+    return in_order(blocks, concat_dim)
 
 
 def passed_along(block, axis, distance):
@@ -73,7 +95,7 @@
 
 
 def per_device(latent, w_in, b_in, gain, w_mid, b_mid, w_time, b_time):
-    owned = lax.all_to_all(latent, "tm", split_axis=0, concat_axis=1, tiled=True)
+    owned = exchange_in_pairs(latent, "tm", 0, 1)
     frames = owned.shape[0]
     lat = owned.reshape(frames, H, W, ZC)
     earlier = passed_along(lat, "tm", 1)

time: 155 us -> 194 us (1.25)
  waiting for transfers between devices: 26.8 us -> 54 us
  starting transfers between devices: 6 us -> 27.7 us
  blocking collectives: 11.1 us -> 0 us
    ppermute x0 -> x15, waiting for transfers between devices: none -> 27.6 us  [exchange_in_pairs(): outs.append(lax.ppermute(sent, axis, [(i, i ^ step) for i in range(size)]))]
    ppermute x0 -> x15, starting transfers between devices: none -> 21.4 us  [exchange_in_pairs(): outs.append(lax.ppermute(sent, axis, [(i, i ^ step) for i in range(size)]))]
    all_to_all x1 -> x0, blocking collectives: 11.1 us -> none  [per_device(): lax.all_to_all(latent, 'tm', split_axis=0, concat_axis=1, tiled=True)]
    unnamed x121 -> x135, local copies, waits for them, and re-layouts: 16.8 us -> 17 us
  transfers between devices with their start and end apart: 3 -> 18, of which waited for: 3 -> 14; matrix products, arithmetic and copies ran while one was open for 3% -> 2% of each run, Pallas kernels for 0% -> 0%
where the time goes in v1:
time: 194 us; the launch traced here: 193 us
  matrix products  59.4 us (31%)
  waiting for transfers between devices  54 us (28%)
  local copies, waits for them, and re-layouts  50.5 us (26%)
  starting transfers between devices  27.7 us (14%)
    dot_general x30, matrix products, conv_valid(): jnp.dot(window.reshape(-1, inner), kernel, preferred_element_type=jnp.flo...  57.4 us
    ppermute x15, waiting for transfers between devices, exchange_in_pairs(): outs.append(lax.ppermute(sent, axis, [(i, i ^ step) for i in range(size)]))  27.6 us
    ppermute x3, waiting for transfers between devices, passed_along(): return lax.ppermute(block, axis, route)  26.5 us
    ppermute x15, starting transfers between devices, exchange_in_pairs(): outs.append(lax.ppermute(sent, axis, [(i, i ^ step) for i in range(size)]))  21.4 us
    concatenate x29, local copies, waits for them, and re-layouts, conv_input(): jnp.concatenate(windows, axis=-1).reshape(frames * rows * cols, 27 * inner)  18.7 us
    unnamed x135, local copies, waits for them, and re-layouts  17 us
    slice x2, local copies, waits for them, and re-layouts, conv_valid(): padded[step_t:step_t + frames, step_h:step_h + rows, step_w:step_w + cols...  8.33 us
    ppermute x3, starting transfers between devices, passed_along(): return lax.ppermute(block, axis, route)  6.28 us
  transfers between devices with their start and end apart: 18, of which 14 were waited for; matrix products, arithmetic and copies ran while one was open for 2% of the time, Pallas kernels for 0%

profile of v1, /device:TPU:8, one launch (start us, length us, event | category | flops | bytes accessed | tf_op | source)
XLA Modules:
  0.0 193.5 jit_solution(632017568949623640)
XLA Ops:
  1.0 2.0 %collective-permute-start.14 = (bf16[2,512]{1,0:T(2,128)(2,1)S(1)}, bf16[2,512]{1,0:T(2,128)(2,1)S(1)}, u32[]{:S(2)}, u32[]{:S(2)}) collective-permute-start(bf16[2,512]{1,0:T(2,128)(2,1)S(1)} %get-tuple-element.54), channel_id=1, source_target_pairs={{0,15},{1,14},{2,13},{3,12},{4,11},{5,10},{6,9},{7,8},{8,7},{9,6},... | collective-permute-start | bytes 6152 | tf_op jit(solution)/shard_map/ppermute | solution.py:29
  8.2 2.1 %collective-permute-done.1 = bf16[2,512]{1,0:T(2,128)(2,1)S(1)} collective-permute-done((bf16[2,512]{1,0:T(2,128)(2,1)S(1)}, bf16[2,512]{1,0:T(2,128)(2,1)S(1)}, u32[]{:S(2)}, u32[]{:S(2)}) %collective-permute-start.1) | collective-permute-done | bytes 2080 | tf_op jit(solution)/shard_map/ppermute | solution.py:29
  10.4 2.9 %collective-permute-done.2 = bf16[2,512]{1,0:T(2,128)(2,1)S(1)} collective-permute-done((bf16[2,512]{1,0:T(2,128)(2,1)S(1)}, bf16[2,512]{1,0:T(2,128)(2,1)S(1)}, u32[]{:S(2)}, u32[]{:S(2)}) %collective-permute-start.2) | collective-permute-done | bytes 2080 | tf_op jit(solution)/shard_map/ppermute | solution.py:29
  13.2 4.2 %collective-permute-start.3 = (bf16[2,512]{1,0:T(2,128)(2,1)S(1)}, bf16[2,512]{1,0:T(2,128)(2,1)S(1)}, u32[]{:S(2)}, u32[]{:S(2)}) collective-permute-start(bf16[2,512]{1,0:T(2,128)(2,1)S(1)} %get-tuple-element.65), channel_id=1, source_target_pairs={{0,4},{1,5},{2,6},{3,7},{4,0},{5,1},{6,2},{7,3},{8,12},{9,13},{10,... | collective-permute-start | bytes 6152 | tf_op jit(solution)/shard_map/ppermute | solution.py:29
  19.2 2.7 %collective-permute-done.4 = bf16[2,512]{1,0:T(2,128)(2,1)S(1)} collective-permute-done((bf16[2,512]{1,0:T(2,128)(2,1)S(1)}, bf16[2,512]{1,0:T(2,128)(2,1)S(1)}, u32[]{:S(2)}, u32[]{:S(2)}) %collective-permute-start.4) | collective-permute-done | bytes 2080 | tf_op jit(solution)/shard_map/ppermute | solution.py:29
  22.0 2.9 %collective-permute-start.5 = (bf16[2,512]{1,0:T(2,128)(2,1)S(1)}, bf16[2,512]{1,0:T(2,128)(2,1)S(1)}, u32[]{:S(2)}, u32[]{:S(2)}) collective-permute-start(bf16[2,512]{1,0:T(2,128)(2,1)S(1)} %get-tuple-element.63), channel_id=1, source_target_pairs={{0,6},{1,7},{2,4},{3,5},{4,2},{5,3},{6,0},{7,1},{8,14},{9,15},{10,... | collective-permute-start | bytes 6152 | tf_op jit(solution)/shard_map/ppermute | solution.py:29
  26.5 3.9 %collective-permute-done.6 = bf16[2,512]{1,0:T(2,128)(2,1)S(1)} collective-permute-done((bf16[2,512]{1,0:T(2,128)(2,1)S(1)}, bf16[2,512]{1,0:T(2,128)(2,1)S(1)}, u32[]{:S(2)}, u32[]{:S(2)}) %collective-permute-start.6) | collective-permute-done | bytes 2080 | tf_op jit(solution)/shard_map/ppermute | solution.py:29
  30.4 4.0 %collective-permute-start.7 = (bf16[2,512]{1,0:T(2,128)(2,1)S(1)}, bf16[2,512]{1,0:T(2,128)(2,1)S(1)}, u32[]{:S(2)}, u32[]{:S(2)}) collective-permute-start(bf16[2,512]{1,0:T(2,128)(2,1)S(1)} %get-tuple-element.61), channel_id=1, source_target_pairs={{0,8},{1,9},{2,10},{3,11},{4,12},{5,13},{6,14},{7,15},{8,0},{9,1},... | collective-permute-start | bytes 6152 | tf_op jit(solution)/shard_map/ppermute | solution.py:29
  36.0 3.9 %collective-permute-done.8 = bf16[2,512]{1,0:T(2,128)(2,1)S(1)} collective-permute-done((bf16[2,512]{1,0:T(2,128)(2,1)S(1)}, bf16[2,512]{1,0:T(2,128)(2,1)S(1)}, u32[]{:S(2)}, u32[]{:S(2)}) %collective-permute-start.8) | collective-permute-done | bytes 2080 | tf_op jit(solution)/shard_map/ppermute | solution.py:29
  39.9 3.9 %collective-permute-start.9 = (bf16[2,512]{1,0:T(2,128)(2,1)S(1)}, bf16[2,512]{1,0:T(2,128)(2,1)S(1)}, u32[]{:S(2)}, u32[]{:S(2)}) collective-permute-start(bf16[2,512]{1,0:T(2,128)(2,1)S(1)} %get-tuple-element.59), channel_id=1, source_target_pairs={{0,10},{1,11},{2,8},{3,9},{4,14},{5,15},{6,12},{7,13},{8,2},{9,3},... | collective-permute-start | bytes 6152 | tf_op jit(solution)/shard_map/ppermute | solution.py:29
  45.3 4.8 %collective-permute-done.10 = bf16[2,512]{1,0:T(2,128)(2,1)S(1)} collective-permute-done((bf16[2,512]{1,0:T(2,128)(2,1)S(1)}, bf16[2,512]{1,0:T(2,128)(2,1)S(1)}, u32[]{:S(2)}, u32[]{:S(2)}) %collective-permute-start.10) | collective-permute-done | bytes 2080 | tf_op jit(solution)/shard_map/ppermute | solution.py:29
  51.1 2.3 %collective-permute-start.15 = (bf16[2,16,32,16]{3,2,1,0:T(8,128)(2,1)S(1)}, bf16[2,16,32,16]{3,2,1,0:T(8,128)(2,1)S(1)}, u32[]{:S(2)}, u32[]{:S(2)}) collective-permute-start(bf16[2,16,32,16]{3,2,1,0:T(8,128)(2,1)S(1)} %reshape_reshape.4), channel_id=1, source_target_pairs={{0,1},{1,2},{2,3},{3,4},{4,5},{5,6},{6,7},{7,8},{8,9},{9,10},{10,1... | collective-permute-start | bytes 98312 | tf_op jit(solution)/shard_map/ppermute | solution.py:37
  53.7 5.9 %collective-permute-done.15 = bf16[2,16,32,16]{3,2,1,0:T(8,128)(2,1)S(1)} collective-permute-done((bf16[2,16,32,16]{3,2,1,0:T(8,128)(2,1)S(1)}, bf16[2,16,32,16]{3,2,1,0:T(8,128)(2,1)S(1)}, u32[]{:S(2)}, u32[]{:S(2)}) %collective-permute-start.15) | collective-permute-done | bytes 32800 | tf_op jit(solution)/shard_map/ppermute | solution.py:37
  60.1 2.5 %pad_slice_fusion.26 = (bf16[2,16,32,16]{3,2,1,0:T(8,128)(2,1)}, bf16[2,16,32,16]{3,2,1,0:T(8,128)(2,1)}, bf16[2,16,32,16]{3,2,1,0:T(8,128)(2,1)}, bf16[2,16,32,...) fusion(bf16[4,16,32,16]{3,2,1,0:T(8,128)(2,1)S(1)} %constant_dy, ...), kind=kLoop, calls=%fused_computation.37 | loop fusion | bytes 688128 | tf_op jit(solution)/shard_map/slice | solution.py:80
  97.3 2.0 %multiply_reduce_fusion = (f32[1024]{0:T(1024)S(1)}, f32[1024,384]{1,0:T(8,128)S(1)}) fusion(f32[384]{0:T(512)S(1)} %copy-done.44, bf16[1024,432]{0,1:T(8,128)(2,1)} %constant_dynamic-update-slice_fusion.18, bf16[432,384]{1,0:T(8,128)(2,1)S(1)} %bitcast.242), kind=kOutput, calls=%fused_computation.34 | convolution fusion | flops 341703680 | bytes 2795008 | tf_op jit(solution)/shard_map/dot_general | solution.py:85
  99.9 1.9 collective-permute-start.16
  101.9 3.0 %fusion.3 = f32[1024,384]{1,0:T(8,128)} fusion(f32[1024,384]{1,0:T(8,128)S(1)} %get-tuple-element.71, f32[384]{0:T(512)S(1)} %copy-done.43, f32[1024]{0:T(1024)S(1)} %add_rsqrt_fusion, bf16[3,3,3,384,384]{4,3,2,1,0:T(8,128)(2,1)} %param.12), kind=kOutput, calls=%fused_computation.64 | convolution fusion | flops 304742400 | bytes 3446272 | tf_op jit(solution)/shard_map/dot_general | solution.py:62
  104.9 9.2 %collective-permute-done.16 = bf16[2,16,32,384]{3,2,1,0:T(8,128)(2,1)S(1)} collective-permute-done((bf16[2,16,32,384]{3,2,1,0:T(8,128)(2,1)S(1)}, bf16[2,16,32,384]{3,2,1,0:T(8,128)(2,1)S(1)}, u32[]{:S(2)}, u32[]{:S(2)}) %collective-permute-start.16) | collective-permute-done | bytes 786464 | tf_op jit(solution)/shard_map/ppermute | solution.py:37
  114.3 2.1 %pad_slice_fusion.23 = (bf16[2,16,32,384]{3,2,1,0:T(8,128)(2,1)S(1)}, bf16[2,16,32,384]{3,2,1,0:T(8,128)(2,1)S(1)}, bf16[2,16,32,384]{3,2,1,0:T(8,128)(2,1)S(1)}...) fusion(bf16[4,16,32,384]{3,2,1,0:T(8,128)(2,1)S(1)} %pad_maximum_fusion), kind=kLoop, calls=%fused_computation.24 | loop fusion | bytes 5505024 | tf_op jit(solution)/shard_map/slice | solution.py:55
  116.5 6.2 %pad_slice_fusion = (bf16[2,16,32,384]{3,2,1,0:T(8,128)(2,1)}, bf16[2,16,32,384]{3,2,1,0:T(8,128)(2,1)}, bf16[2,16,32,384]{3,2,1,0:T(8,128)(2,1)}, bf16[2,16,32,...) fusion(bf16[4,16,32,384]{3,2,1,0:T(8,128)(2,1)S(1)} %pad_maximu, ...), kind=kLoop, calls=%fused_computation.1 | loop fusion | bytes 16515072 | tf_op jit(solution)/shard_map/slice | solution.py:55
  130.7 1.8 fusion.57
  132.5 1.8 fusion.55
  134.4 1.9 fusion.51
  136.2 1.8 fusion.49
  139.8 1.8 fusion.45
  152.4 2.0 %fusion.29 = f32[1024,384]{1,0:T(8,128)} fusion(bf16[1024,384]{1,0:T(8,128)(2,1)S(1)} %bitcast.254, bf16[3,3,3,384,384]{4,3,2,1,0:T(8,128)(2,1)S(1)} %bitcast.247), kind=kOutput, calls=%fused_computation.90 | convolution fusion | flops 301989888 | bytes 2654208 | tf_op jit(solution)/shard_map/dot_general | solution.py:62
  154.4 1.9 fusion.27
  156.3 1.8 fusion.25
  158.1 1.8 fusion.23
  161.7 13.2 %add_add_fusion = f32[1024,384]{1,0:T(8,128)S(1)} fusion(f32[1024,384]{1,0:T(8,128)} %fusion.12, f32[1024,384]{1,0:T(8,128)S(1)} %fusion.14, f32[1024,384]{1,0:T(8,128)S(1)} %fusion.16, f32[1024,384]{1,0:T(8,128)} %fusion.3, f32[1024,384]{1,0:T(8,128)S(1)} %fusion.19, f32[1024,384]{1,0:T(8,128)} %fusion.21, f32[1024,384]{1,0:T(8,128)} %fusion.23, ...), kind=kOutput, calls=%fused_computation.31 | convolution fusion | flops 312606720 | bytes 43550208 | tf_op jit(solution)/shard_map/dot_general | solution.py:62
  175.2 2.1 %collective-permute-start.17 = (bf16[2,16,32,384]{3,2,1,0:T(8,128)(2,1)S(1)}, bf16[2,16,32,384]{3,2,1,0:T(8,128)(2,1)S(1)}, u32[]{:S(2)}, u32[]{:S(2)}) collective-permute-start(bf16[2,16,32,384]{3,2,1,0:T(8,128)(2,1)S(1)} %add_convert_fusion.2), channel_id=1, source_target_pairs={{0,1},{1,2},{2,3},{3,4},{4,5},{5,6},{6,7},{7,8},{8,9},{9,10},{10,1... | collective-permute-start | bytes 2359304 | tf_op jit(solution)/shard_map/ppermute | solution.py:37
  178.3 11.3 %collective-permute-done.17 = bf16[2,16,32,384]{3,2,1,0:T(8,128)(2,1)S(1)} collective-permute-done((bf16[2,16,32,384]{3,2,1,0:T(8,128)(2,1)S(1)}, bf16[2,16,32,384]{3,2,1,0:T(8,128)(2,1)S(1)}, u32[]{:S(2)}, u32[]{:S(2)}) %collective-permute-start.17) | collective-permute-done | bytes 786464 | tf_op jit(solution)/shard_map/ppermute | solution.py:37
  (222 shorter events, 77.2 us)
Async XLA Ops:
  0.0 97.3 %copy-start = (bf16[3,3,3,16,384]{4,3,2,1,0:T(8,128)(2,1)S(1)}, bf16[3,3,3,16,384]{4,3,2,1,0:T(8,128)(2,1)}, u32[]{:S(2)}) copy-start(bf16[3,3,3,16,384]{4,3,2,1,0:T(8,128)(2,1)} %param.9) | copy-start | bytes 995332
  1.0 49.2 %collective-permute-start.14 = (bf16[2,512]{1,0:T(2,128)(2,1)S(1)}, bf16[2,512]{1,0:T(2,128)(2,1)S(1)}, u32[]{:S(2)}, u32[]{:S(2)}) collective-permute-start(bf16[2,512]{1,0:T(2,128)(2,1)S(1)} %get-tuple-element.54), channel_id=1, source_target_pairs={{0,15},{1,14},{2,13},{3,12},{4,11},{5,10},{6,9},{7,8},{8,7},{9,6},... | collective-permute-start | bytes 6152 | tf_op jit(solution)/shard_map/ppermute | solution.py:29
  3.0 47.1 %collective-permute-start.13 = (bf16[2,512]{1,0:T(2,128)(2,1)S(1)}, bf16[2,512]{1,0:T(2,128)(2,1)S(1)}, u32[]{:S(2)}, u32[]{:S(2)}) collective-permute-start(bf16[2,512]{1,0:T(2,128)(2,1)S(1)} %get-tuple-element.55), channel_id=1, source_target_pairs={{0,14},{1,15},{2,12},{3,13},{4,10},{5,11},{6,8},{7,9},{8,6},{9,7},... | collective-permute-start | bytes 6152 | tf_op jit(solution)/shard_map/ppermute | solution.py:29
  3.7 46.5 %collective-permute-start.12 = (bf16[2,512]{1,0:T(2,128)(2,1)S(1)}, bf16[2,512]{1,0:T(2,128)(2,1)S(1)}, u32[]{:S(2)}, u32[]{:S(2)}) collective-permute-start(bf16[2,512]{1,0:T(2,128)(2,1)S(1)} %get-tuple-element.56), channel_id=1, source_target_pairs={{0,13},{1,12},{2,15},{3,14},{4,9},{5,8},{6,11},{7,10},{8,5},{9,4},... | collective-permute-start | bytes 6152 | tf_op jit(solution)/shard_map/ppermute | solution.py:29
  5.0 45.1 %collective-permute-start.11 = (bf16[2,512]{1,0:T(2,128)(2,1)S(1)}, bf16[2,512]{1,0:T(2,128)(2,1)S(1)}, u32[]{:S(2)}, u32[]{:S(2)}) collective-permute-start(bf16[2,512]{1,0:T(2,128)(2,1)S(1)} %get-tuple-element.57), channel_id=1, source_target_pairs={{0,12},{1,13},{2,14},{3,15},{4,8},{5,9},{6,10},{7,11},{8,4},{9,5},... | collective-permute-start | bytes 6152 | tf_op jit(solution)/shard_map/ppermute | solution.py:29
  5.5 1.2 collective-permute-start
  6.6 3.6 %collective-permute-start.1 = (bf16[2,512]{1,0:T(2,128)(2,1)S(1)}, bf16[2,512]{1,0:T(2,128)(2,1)S(1)}, u32[]{:S(2)}, u32[]{:S(2)}) collective-permute-start(bf16[2,512]{1,0:T(2,128)(2,1)S(1)} %get-tuple-element.67), channel_id=1, source_target_pairs={{0,2},{1,3},{2,0},{3,1},{4,6},{5,7},{6,4},{7,5},{8,10},{9,11},{10,... | collective-permute-start | bytes 6152 | tf_op jit(solution)/shard_map/ppermute | solution.py:29
  10.2 3.0 %collective-permute-start.2 = (bf16[2,512]{1,0:T(2,128)(2,1)S(1)}, bf16[2,512]{1,0:T(2,128)(2,1)S(1)}, u32[]{:S(2)}, u32[]{:S(2)}) collective-permute-start(bf16[2,512]{1,0:T(2,128)(2,1)S(1)} %get-tuple-element.66), channel_id=1, source_target_pairs={{0,3},{1,2},{2,1},{3,0},{4,7},{5,6},{6,5},{7,4},{8,11},{9,10},{10,... | collective-permute-start | bytes 6152 | tf_op jit(solution)/shard_map/ppermute | solution.py:29
  13.2 5.7 %collective-permute-start.3 = (bf16[2,512]{1,0:T(2,128)(2,1)S(1)}, bf16[2,512]{1,0:T(2,128)(2,1)S(1)}, u32[]{:S(2)}, u32[]{:S(2)}) collective-permute-start(bf16[2,512]{1,0:T(2,128)(2,1)S(1)} %get-tuple-element.65), channel_id=1, source_target_pairs={{0,4},{1,5},{2,6},{3,7},{4,0},{5,1},{6,2},{7,3},{8,12},{9,13},{10,... | collective-permute-start | bytes 6152 | tf_op jit(solution)/shard_map/ppermute | solution.py:29
  18.9 3.0 %collective-permute-start.4 = (bf16[2,512]{1,0:T(2,128)(2,1)S(1)}, bf16[2,512]{1,0:T(2,128)(2,1)S(1)}, u32[]{:S(2)}, u32[]{:S(2)}) collective-permute-start(bf16[2,512]{1,0:T(2,128)(2,1)S(1)} %get-tuple-element.64), channel_id=1, source_target_pairs={{0,5},{1,4},{2,7},{3,6},{4,1},{5,0},{6,3},{7,2},{8,13},{9,12},{10,... | collective-permute-start | bytes 6152 | tf_op jit(solution)/shard_map/ppermute | solution.py:29
  22.0 4.5 %collective-permute-start.5 = (bf16[2,512]{1,0:T(2,128)(2,1)S(1)}, bf16[2,512]{1,0:T(2,128)(2,1)S(1)}, u32[]{:S(2)}, u32[]{:S(2)}) collective-permute-start(bf16[2,512]{1,0:T(2,128)(2,1)S(1)} %get-tuple-element.63), channel_id=1, source_target_pairs={{0,6},{1,7},{2,4},{3,5},{4,2},{5,3},{6,0},{7,1},{8,14},{9,15},{10,... | collective-permute-start | bytes 6152 | tf_op jit(solution)/shard_map/ppermute | solution.py:29
  26.4 3.9 %collective-permute-start.6 = (bf16[2,512]{1,0:T(2,128)(2,1)S(1)}, bf16[2,512]{1,0:T(2,128)(2,1)S(1)}, u32[]{:S(2)}, u32[]{:S(2)}) collective-permute-start(bf16[2,512]{1,0:T(2,128)(2,1)S(1)} %get-tuple-element.62), channel_id=1, source_target_pairs={{0,7},{1,6},{2,5},{3,4},{4,3},{5,2},{6,1},{7,0},{8,15},{9,14},{10,... | collective-permute-start | bytes 6152 | tf_op jit(solution)/shard_map/ppermute | solution.py:29
  30.4 5.6 %collective-permute-start.7 = (bf16[2,512]{1,0:T(2,128)(2,1)S(1)}, bf16[2,512]{1,0:T(2,128)(2,1)S(1)}, u32[]{:S(2)}, u32[]{:S(2)}) collective-permute-start(bf16[2,512]{1,0:T(2,128)(2,1)S(1)} %get-tuple-element.61), channel_id=1, source_target_pairs={{0,8},{1,9},{2,10},{3,11},{4,12},{5,13},{6,14},{7,15},{8,0},{9,1},... | collective-permute-start | bytes 6152 | tf_op jit(solution)/shard_map/ppermute | solution.py:29
  36.0 3.9 %collective-permute-start.8 = (bf16[2,512]{1,0:T(2,128)(2,1)S(1)}, bf16[2,512]{1,0:T(2,128)(2,1)S(1)}, u32[]{:S(2)}, u32[]{:S(2)}) collective-permute-start(bf16[2,512]{1,0:T(2,128)(2,1)S(1)} %get-tuple-element.60), channel_id=1, source_target_pairs={{0,9},{1,8},{2,11},{3,10},{4,13},{5,12},{6,15},{7,14},{8,1},{9,0},... | collective-permute-start | bytes 6152 | tf_op jit(solution)/shard_map/ppermute | solution.py:29
  39.9 5.4 %collective-permute-start.9 = (bf16[2,512]{1,0:T(2,128)(2,1)S(1)}, bf16[2,512]{1,0:T(2,128)(2,1)S(1)}, u32[]{:S(2)}, u32[]{:S(2)}) collective-permute-start(bf16[2,512]{1,0:T(2,128)(2,1)S(1)} %get-tuple-element.59), channel_id=1, source_target_pairs={{0,10},{1,11},{2,8},{3,9},{4,14},{5,15},{6,12},{7,13},{8,2},{9,3},... | collective-permute-start | bytes 6152 | tf_op jit(solution)/shard_map/ppermute | solution.py:29
  45.3 4.8 %collective-permute-start.10 = (bf16[2,512]{1,0:T(2,128)(2,1)S(1)}, bf16[2,512]{1,0:T(2,128)(2,1)S(1)}, u32[]{:S(2)}, u32[]{:S(2)}) collective-permute-start(bf16[2,512]{1,0:T(2,128)(2,1)S(1)} %get-tuple-element.58), channel_id=1, source_target_pairs={{0,11},{1,10},{2,9},{3,8},{4,15},{5,14},{6,13},{7,12},{8,3},{9,2},... | collective-permute-start | bytes 6152 | tf_op jit(solution)/shard_map/ppermute | solution.py:29
  51.1 8.6 %collective-permute-start.15 = (bf16[2,16,32,16]{3,2,1,0:T(8,128)(2,1)S(1)}, bf16[2,16,32,16]{3,2,1,0:T(8,128)(2,1)S(1)}, u32[]{:S(2)}, u32[]{:S(2)}) collective-permute-start(bf16[2,16,32,16]{3,2,1,0:T(8,128)(2,1)S(1)} %reshape_reshape.4), channel_id=1, source_target_pairs={{0,1},{1,2},{2,3},{3,4},{4,5},{5,6},{6,7},{7,8},{8,9},{9,10},{10,1... | collective-permute-start | bytes 98312 | tf_op jit(solution)/shard_map/ppermute | solution.py:37
  64.9 14.1 %copy-start.27 = (bf16[2,16,32,16]{3,2,1,0:T(8,128)(2,1)S(1)}, bf16[2,16,32,16]{3,2,1,0:T(8,128)(2,1)}, u32[]{:S(2)}) copy-start(bf16[2,16,32,16]{3,2,1,0:T(8,128)(2,1)} %get-tuple-element.36) | copy-start | bytes 98308
  65.7 14.1 %copy-start.26 = (bf16[2,16,32,16]{3,2,1,0:T(8,128)(2,1)S(1)}, bf16[2,16,32,16]{3,2,1,0:T(8,128)(2,1)}, u32[]{:S(2)}) copy-start(bf16[2,16,32,16]{3,2,1,0:T(8,128)(2,1)} %get-tuple-element.37) | copy-start | bytes 98308
  66.4 13.5 %copy-start.25 = (bf16[2,16,32,16]{3,2,1,0:T(8,128)(2,1)S(1)}, bf16[2,16,32,16]{3,2,1,0:T(8,128)(2,1)}, u32[]{:S(2)}) copy-start(bf16[2,16,32,16]{3,2,1,0:T(8,128)(2,1)} %get-tuple-element.38) | copy-start | bytes 98308
  66.5 13.5 %copy-start.24 = (bf16[2,16,32,16]{3,2,1,0:T(8,128)(2,1)S(1)}, bf16[2,16,32,16]{3,2,1,0:T(8,128)(2,1)}, u32[]{:S(2)}) copy-start(bf16[2,16,32,16]{3,2,1,0:T(8,128)(2,1)} %get-tuple-element.39) | copy-start | bytes 98308
  67.2 13.0 %copy-start.23 = (bf16[2,16,32,16]{3,2,1,0:T(8,128)(2,1)S(1)}, bf16[2,16,32,16]{3,2,1,0:T(8,128)(2,1)}, u32[]{:S(2)}) copy-start(bf16[2,16,32,16]{3,2,1,0:T(8,128)(2,1)} %get-tuple-element.40) | copy-start | bytes 98308
  68.9 11.4 %copy-start.22 = (bf16[2,16,32,16]{3,2,1,0:T(8,128)(2,1)S(1)}, bf16[2,16,32,16]{3,2,1,0:T(8,128)(2,1)}, u32[]{:S(2)}) copy-start(bf16[2,16,32,16]{3,2,1,0:T(8,128)(2,1)} %get-tuple-element.41) | copy-start | bytes 98308
  70.6 9.8 %copy-start.21 = (bf16[2,16,32,16]{3,2,1,0:T(8,128)(2,1)S(1)}, bf16[2,16,32,16]{3,2,1,0:T(8,128)(2,1)}, u32[]{:S(2)}) copy-start(bf16[2,16,32,16]{3,2,1,0:T(8,128)(2,1)} %get-tuple-element.42) | copy-start | bytes 98308
  80.2 8.5 %copy-start.32 = (bf16[1024,16]{0,1:T(8,128)(2,1)S(1)}, bf16[1024,16]{0,1:T(8,128)(2,1)}, u32[]{:S(2)}) copy-start(bf16[1024,16]{0,1:T(8,128)(2,1)} %copy.81) | copy-start | bytes 98308
  80.4 13.2 %copy-start.31 = (bf16[1024,16]{0,1:T(8,128)(2,1)S(1)}, bf16[1024,16]{0,1:T(8,128)(2,1)}, u32[]{:S(2)}) copy-start(bf16[1024,16]{0,1:T(8,128)(2,1)} %copy.89) | copy-start | bytes 98308
  80.4 14.4 %copy-start.29 = (bf16[1024,16]{0,1:T(8,128)(2,1)S(1)}, bf16[1024,16]{0,1:T(8,128)(2,1)}, u32[]{:S(2)}) copy-start(bf16[1024,16]{0,1:T(8,128)(2,1)} %copy.90) | copy-start | bytes 98308
  80.6 14.9 %copy-start.28 = (bf16[1024,16]{0,1:T(8,128)(2,1)S(1)}, bf16[1024,16]{0,1:T(8,128)(2,1)}, u32[]{:S(2)}) copy-start(bf16[1024,16]{0,1:T(8,128)(2,1)} %copy.91) | copy-start | bytes 98308
  80.6 16.1 %copy-start.30 = (bf16[1024,16]{0,1:T(8,128)(2,1)S(1)}, bf16[1024,16]{0,1:T(8,128)(2,1)}, u32[]{:S(2)}) copy-start(bf16[1024,16]{0,1:T(8,128)(2,1)} %copy.93) | copy-start | bytes 98308
  80.6 16.7 %copy-start.44 = (f32[384]{0:T(512)S(1)}, f32[384]{0:T(512)}, u32[]{:S(2)}) copy-start(f32[384]{0:T(512)} %param.10) | copy-start | bytes 4612
  99.9 14.2 %collective-permute-start.16 = (bf16[2,16,32,384]{3,2,1,0:T(8,128)(2,1)S(1)}, bf16[2,16,32,384]{3,2,1,0:T(8,128)(2,1)S(1)}, u32[]{:S(2)}, u32[]{:S(2)}) collective-permute-start(bf16[2,16,32,384]{3,2,1,0:T(8,128)(2,1)S(1)} %multiply_convert_fusion.1), channel_id=1, source_target_pairs={{0,1},{1,2},{2,3},{3,4},{4,5},{5,6},{6,7},{7,8},{8,9},{9,10},{10,1... | collective-permute-start | bytes 2359304 | tf_op jit(solution)/shard_map/ppermute | solution.py:37
  175.2 14.3 %collective-permute-start.17 = (bf16[2,16,32,384]{3,2,1,0:T(8,128)(2,1)S(1)}, bf16[2,16,32,384]{3,2,1,0:T(8,128)(2,1)S(1)}, u32[]{:S(2)}, u32[]{:S(2)}) collective-permute-start(bf16[2,16,32,384]{3,2,1,0:T(8,128)(2,1)S(1)} %add_convert_fusion.2), channel_id=1, source_target_pairs={{0,1},{1,2},{2,3},{3,4},{4,5},{5,6},{6,7},{7,8},{8,9},{9,10},{10,1... | collective-permute-start | bytes 2359304 | tf_op jit(solution)/shard_map/ppermute | solution.py:37
  (33 other events, 82.7 us)
